TPU v7x, 512 devices: a whole 4x8x8 slice. The times are simulated.
512 devices in a mesh: dp: 64 (over x, y, core), code: 8 (over z).
Axes of the slice: x: 4, y: 8, z: 8, core: 2. Of those that a mesh axis runs over, the one named last changes fastest.
Arguments:
- items: float32 [65536, 512], P(('dp', 'code')), may hold values from -6 to 6
- codewords: float32 [8192, 512], P('code'), may hold values from -6 to 6
- assign: int32 [65536], P('dp'), may hold values from 0 to 8191, as said below
Outputs:
- new_codewords: float32 [8192, 512], P('code', 'dp')
- residual: float32 [65536, 512], P(('dp', 'code'))
Inputs may be any that keep to these rules, and one draw needn't show every extreme that they name: `assign`: the items are laid out in aligned blocks of 128 (the items of one device). Splitting the codewords into equal ranges, one per index of code, the items of one block name codewords of exactly half of the ranges, 32 items for each such range.
All inputs are finite; a program needn't handle non-finite values.
Results may differ from a plain program's by a relative error of at most 0.0003.
Values sent between devices are 32-bit elements; how exact they have to be, the bound alone decides.
No kernel may reach another device: no remote copies, remote signals or barrier semaphores. Data moves between devices by JAX's collectives and lax.ppermute only.
A program may use at most 64 MiB of HBM per device.

v0:
```python
import jax
import jax.numpy as jnp
from jax import lax
from jax.sharding import Mesh, PartitionSpec as P

K = 8192
ITERS = 3
DP = ("x", "y", "core")
epsilon = 1e-05
inverse_temp = 64.0


def unit_rows(values):
    return values * lax.rsqrt(jnp.mean(values * values, axis=-1, keepdims=True) + epsilon)


def exchange_sum(part, axes):
    count = lax.axis_size(axes)
    copies = jnp.broadcast_to(part[None], (count,) + part.shape)
    return jnp.sum(lax.all_to_all(copies, axes, 0, 0), axis=0)


def scatter_sum(blocks, axis):
    return jnp.sum(lax.all_to_all(blocks, axis, 0, 0), axis=0)


def body(items, codewords, assign):
    code_count = lax.axis_size("code")
    dp_count = lax.axis_size(DP)
    local_codes = codewords.shape[0]
    own_rows, width = items.shape
    total_items = own_rows * code_count * dp_count
    scaled = unit_rows(codewords) * (inverse_temp / width)
    gathered = lax.all_gather(items, "code", axis=0, tiled=True)
    logits = lax.dot_general(
        unit_rows(gathered),
        scaled,
        (((1,), (1,)), ((), ())),
        precision=lax.Precision.HIGH,
        preferred_element_type=jnp.float32,
    )
    kernel_vals = jnp.exp(logits)
    col_part = jnp.sum(kernel_vals, axis=0)
    for _ in range(ITERS):
        col_scale = 1.0 / (K * exchange_sum(col_part, DP))
        row_part = jnp.sum(kernel_vals * col_scale[None, :], axis=1)
        row_scale = 1.0 / (total_items * exchange_sum(row_part, "code"))
        col_part = jnp.sum(kernel_vals * row_scale[:, None], axis=0)
    mass = exchange_sum(col_part, DP)
    nx, ny, nc = (lax.axis_size("x"), lax.axis_size("y"), lax.axis_size("core"))
    cols = width // dp_count
    numerator = lax.dot_general(
        row_scale[:, None] * gathered,
        kernel_vals,
        (((0,), (0,)), ((), ())),
        precision=lax.Precision.HIGH,
        preferred_element_type=jnp.float32,
    )
    halves = numerator.reshape(nx * ny, nc, cols, local_codes)
    core = lax.axis_index("core")
    mine = lax.dynamic_index_in_dim(halves, core, 1, keepdims=False)
    other = lax.dynamic_index_in_dim(halves, 1 - core, 1, keepdims=False)
    chip = mine + lax.ppermute(other, "core", [(0, 1), (1, 0)])
    owned = scatter_sum(chip.reshape(nx, ny, cols, local_codes), "x")
    owned = scatter_sum(owned, "y")
    new_codewords = (owned / mass[None, :]).T
    my_code = lax.axis_index("code")
    offset = my_code * local_codes
    index_rows = assign - offset
    inside = (index_rows >= 0) & (index_rows < local_codes)
    picked = jnp.take(codewords, jnp.clip(index_rows, 0, local_codes - 1), axis=0)
    looked = lax.psum_scatter(
        jnp.where(inside[:, None], picked, jnp.float32(0.0)),
        "code",
        scatter_dimension=0,
        tiled=True,
    )
    residual = items - looked
    return (new_codewords, residual)


def solution(mesh):
    cores = 2
    ny = 8
    dp, code = mesh.devices.shape
    fine = Mesh(
        mesh.devices.reshape(dp // (ny * cores), ny, cores, code), ("x", "y", "core", "code")
    )
    in_specs = (P(DP + ("code",), None), P("code", None), P(DP))
    out_specs = (P("code", DP), P(DP + ("code",), None))
    return jax.shard_map(body, mesh=fine, in_specs=in_specs, out_specs=out_specs, check_vma=False)
```

profile of v0, /device:TPU:1, one launch (start us, length us, event | category | flops | bytes accessed | tf_op | source)
XLA Modules:
  0.0 254.8 jit_solution(13360606303036772084)
XLA Ops:
  9.9 46.3 %all-gather.2.cloned.1.call-done = f32[1024,512]{1,0:T(8,128)} async-done(((f32[128,512]{1,0:T(8,128)}), f32[1024,512]{1,0:T(8,128)}) %all-gather.2.cloned.1.call-update) | async-done | bytes 2097168 | tf_op jit(solution)/shard_map/all_gather | solution.py:34
  58.4 5.6 %exponential_reduce_fusion = (f32[1024]{0:T(1024)S(1)}, f32[1024,1024]{1,0:T(8,128)}) fusion(f32[1024,512]{1,0:T(8,128)S(1)} %copy-done, f32[1024]{0:T(1024)S(1)} %add_rsqrt_fusion, f32[1024,512]{1,0:T(8,128)S(1)} %copy-done.1, f32[1024]{0:T(1024)S(1)} %add_rsqrt_fusion.1), kind=kOutput, calls=%fused_computation.9 | convolution fusion | flops 3223845888 | bytes 8400896 | tf_op jit(solution)/shard_map/dot_general | solution.py:35
  64.1 26.2 %all_to_all.52 = f32[64,1,1024]{2,1,0:T(1,128)S(1)} all-to-all(f32[64,1,1024]{2,1,0:T(1,128)S(1)} %broadcast_in_dim.31), channel_id=1, replica_groups=mesh['x'=4,'y'=8,'core'=2,'code'=8] {'x','y','core'}, dimensions={0} | all-to-all | bytes 524288 | tf_op jit(solution)/shard_map/all_to_all | solution.py:20
  90.5 2.9 %multiply_reduce_fusion.5 = f32[1024]{0:T(1024)S(1)} fusion(f32[1024,1024]{1,0:T(8,128)} %get-tuple-element.5, f32[1024]{0:T(1024)S(1)} %multiply_divide_fusion.5), kind=kLoop, calls=%fused_computation.6 | loop fusion | flops 2096128 | bytes 4202496 | tf_op jit(solution)/shard_map/reduce_sum | solution.py:46
  93.4 10.5 %all_to_all.53 = f32[8,1,1024]{2,1,0:T(1,128)S(1)} all-to-all(f32[8,1,1024]{2,1,0:T(1,128)S(1)} %broadcast_in_dim.32), channel_id=1, replica_groups=mesh['x'=4,'y'=8,'core'=2,'code'=8] {'code'}, dimensions={0} | all-to-all | bytes 65536 | tf_op jit(solution)/shard_map/all_to_all | solution.py:20
  107.7 7.5 %all-to-all-start.2 = ((f32[64,1,1024]{2,1,0:T(1,128)}), f32[64,1,1024]{2,1,0:T(1,128)S(1)}, u32[]{:S(2)}, u32[]{:S(2)}) async-start(f32[64,1,1024]{2,1,0:T(1,128)} %broadcast_in_dim.33), calls=%async_computation.2 | async-start | bytes 524288 | tf_op jit(solution)/shard_map/all_to_all | solution.py:20
  115.1 12.0 %all-to-all-done.2 = f32[64,1,1024]{2,1,0:T(1,128)S(1)} async-done(((f32[64,1,1024]{2,1,0:T(1,128)}), f32[64,1,1024]{2,1,0:T(1,128)S(1)}, u32[]{:S(2)}, u32[]{:S(2)}) %all-to-all-start.2) | async-done | bytes 262176 | tf_op jit(solution)/shard_map/all_to_all | solution.py:20
  127.3 2.9 %multiply_reduce_fusion.3 = f32[1024]{0:T(1024)S(1)} fusion(f32[1024,1024]{1,0:T(8,128)} %get-tuple-element.5, f32[1024]{0:T(1024)S(1)} %multiply_divide_fusion.3), kind=kLoop, calls=%fused_computation.4 | loop fusion | flops 2096128 | bytes 4202496 | tf_op jit(solution)/shard_map/reduce_sum | solution.py:46
  130.8 3.3 %all-to-all-start.3 = ((f32[8,1,1024]{2,1,0:T(1,128)}), f32[8,1,1024]{2,1,0:T(1,128)S(1)}, u32[]{:S(2)}, u32[]{:S(2)}) async-start(f32[8,1,1024]{2,1,0:T(1,128)} %broadcast_in_dim.34), calls=%async_computation.3 | async-start | bytes 65536 | tf_op jit(solution)/shard_map/all_to_all | solution.py:20
  134.2 4.9 %gather_fusion = f32[1024,512]{1,0:T(8,128)} fusion(f32[1024,512]{1,0:T(8,128)S(1)} %copy-done, s32[1024]{0:T(1024)S(1)} %fusion.11), kind=kCustom, calls=%fused_computation | custom fusion | bytes 4198400 | tf_op jit(solution)/shard_map/jit(_take)/gather | solution.py:71
  141.0 2.9 %multiply_reduce_fusion.2 = f32[1024]{0:T(1024)S(1)} fusion(f32[1024,1024]{1,0:T(8,128)} %get-tuple-element.5, f32[1024]{0:T(1024)S(1)} %multiply_divide_fusion.2), kind=kLoop, calls=%fused_computation.3 | loop fusion | flops 2096128 | bytes 4202496 | tf_op jit(solution)/shard_map/reduce_sum | solution.py:48
  144.8 7.2 %all-to-all-start.4 = ((f32[64,1,1024]{2,1,0:T(1,128)}), f32[64,1,1024]{2,1,0:T(1,128)S(1)}, u32[]{:S(2)}, u32[]{:S(2)}) async-start(f32[64,1,1024]{2,1,0:T(1,128)} %broadcast_in_dim.35), calls=%async_computation.4 | async-start | bytes 524288 | tf_op jit(solution)/shard_map/all_to_all | solution.py:20
  154.1 9.9 %all-to-all-done.4 = f32[64,1,1024]{2,1,0:T(1,128)S(1)} async-done(((f32[64,1,1024]{2,1,0:T(1,128)}), f32[64,1,1024]{2,1,0:T(1,128)S(1)}, u32[]{:S(2)}, u32[]{:S(2)}) %all-to-all-start.4) | async-done | bytes 262176 | tf_op jit(solution)/shard_map/all_to_all | solution.py:20
  164.2 3.0 %multiply_reduce_fusion.1 = f32[1024]{0:T(1024)S(1)} fusion(f32[1024,1024]{1,0:T(8,128)} %get-tuple-element.5, f32[1024]{0:T(1024)S(1)} %multiply_divide_fusion.1), kind=kLoop, calls=%fused_computation.2 | loop fusion | flops 2096128 | bytes 4202496 | tf_op jit(solution)/shard_map/reduce_sum | solution.py:46
  167.9 3.8 %all-to-all-start.5 = ((f32[8,1,1024]{2,1,0:T(1,128)}), f32[8,1,1024]{2,1,0:T(1,128)S(1)}, u32[]{:S(2)}, u32[]{:S(2)}) async-start(f32[8,1,1024]{2,1,0:T(1,128)} %broadcast_in_dim.36), calls=%async_computation.5 | async-start | bytes 65536 | tf_op jit(solution)/shard_map/all_to_all | solution.py:20
  171.7 7.1 %all-to-all-done.5 = f32[8,1,1024]{2,1,0:T(1,128)S(1)} async-done(((f32[8,1,1024]{2,1,0:T(1,128)}), f32[8,1,1024]{2,1,0:T(1,128)S(1)}, u32[]{:S(2)}, u32[]{:S(2)}) %all-to-all-start.5) | async-done | bytes 32800 | tf_op jit(solution)/shard_map/all_to_all | solution.py:20
  178.9 6.0 %fusion = f32[512,1024]{1,0:T(8,128)S(1)} fusion(f32[1024,1024]{1,0:T(8,128)} %get-tuple-element.5, f32[1024,512]{1,0:T(8,128)S(1)} %copy-done.2, f32[1024]{0:T(1024)S(1)} %multiply_divide_fusion), kind=kOutput, calls=%fused_computation.7 | convolution fusion | flops 3221749760 | bytes 8392704 | tf_op jit(solution)/shard_map/dot_general | solution.py:52
  186.3 3.8 %collective-permute-start = (f32[32,8,1024]{2,1,0:T(8,128)S(1)}, f32[32,8,1024]{2,1,0:T(8,128)S(1)}, u32[]{:S(2)}, u32[]{:S(2)}) collective-permute-start(f32[32,8,1024]{2,1,0:T(8,128)S(1)} %dynamic-slice_bitcast_fusion), channel_id=1, source_target_pairs={{0,8},{8,0},{1,9},{9,1},{2,10},{10,2},{3,11},{11,3},{4,12},{12,4},... | collective-permute-start | bytes 3145736 | tf_op jit(solution)/shard_map/ppermute | solution.py:63
  194.8 3.9 %all-to-all-start.6 = ((f32[4,8,8,1024]{3,2,1,0:T(8,128)}), f32[4,8,8,1024]{3,2,1,0:T(8,128)S(1)}, u32[]{:S(2)}, u32[]{:S(2)}) async-start(f32[4,8,8,1024]{3,2,1,0:T(8,128)} %bitcast.3), calls=%async_computation.6 | async-start | bytes 2097152 | tf_op jit(solution)/shard_map/all_to_all | solution.py:24
  201.5 11.7 %all-to-all-done.6 = f32[4,8,8,1024]{3,2,1,0:T(8,128)S(1)} async-done(((f32[4,8,8,1024]{3,2,1,0:T(8,128)}), f32[4,8,8,1024]{3,2,1,0:T(8,128)S(1)}, u32[]{:S(2)}, u32[]{:S(2)}) %all-to-all-start.6) | async-done | bytes 1048608 | tf_op jit(solution)/shard_map/all_to_all | solution.py:24
  214.1 6.5 %all-to-all-start.8 = ((f32[64,1,1024]{2,1,0:T(1,128)}), f32[64,1,1024]{2,1,0:T(1,128)S(1)}, u32[]{:S(2)}, u32[]{:S(2)}) async-start(f32[64,1,1024]{2,1,0:T(1,128)} %broadcast_in_dim.37), calls=%async_computation.8 | async-start | bytes 524288 | tf_op jit(solution)/shard_map/all_to_all | solution.py:20
  221.3 11.2 %all-to-all-done.8 = f32[64,1,1024]{2,1,0:T(1,128)S(1)} async-done(((f32[64,1,1024]{2,1,0:T(1,128)}), f32[64,1,1024]{2,1,0:T(1,128)S(1)}, u32[]{:S(2)}, u32[]{:S(2)}) %all-to-all-start.8) | async-done | bytes 262176 | tf_op jit(solution)/shard_map/all_to_all | solution.py:20
  232.5 3.9 %all-to-all-start.7 = ((f32[8,8,1024]{2,1,0:T(8,128)}), f32[8,8,1024]{2,1,0:T(8,128)S(1)}, u32[]{:S(2)}, u32[]{:S(2)}) async-start(f32[8,8,1024]{2,1,0:T(8,128)} %reduce_sum.176), calls=%async_computation.7 | async-start | bytes 524288 | tf_op jit(solution)/shard_map/all_to_all | solution.py:24
  238.3 9.0 %all-to-all-done.7 = f32[8,8,1024]{2,1,0:T(8,128)S(1)} async-done(((f32[8,8,1024]{2,1,0:T(8,128)}), f32[8,8,1024]{2,1,0:T(8,128)S(1)}, u32[]{:S(2)}, u32[]{:S(2)}) %all-to-all-start.7) | async-done | bytes 262176 | tf_op jit(solution)/shard_map/all_to_all | solution.py:24
  (56 shorter events, 28.5 us)
Async XLA Ops:
  7.2 49.0 %all-gather.2.cloned.1.call-start = ((), (), s32[]{:S(2)}) async-start(), calls=%async_computation.10 | async-start | bytes 2359296 | tf_op jit(solution)/shard_map/all_gather | solution.py:34
  7.9 50.3 %copy-start = (f32[1024,512]{1,0:T(8,128)S(1)}, f32[1024,512]{1,0:T(8,128)}, u32[]{:S(2)}) copy-start(f32[1024,512]{1,0:T(8,128)} %param.4) | copy-start | bytes 6291460
  56.2 2.2 copy-start.1
  107.7 19.5 %all-to-all-start.2 = ((f32[64,1,1024]{2,1,0:T(1,128)}), f32[64,1,1024]{2,1,0:T(1,128)S(1)}, u32[]{:S(2)}, u32[]{:S(2)}) async-start(f32[64,1,1024]{2,1,0:T(1,128)} %broadcast_in_dim.33), calls=%async_computation.2 | async-start | bytes 524288 | tf_op jit(solution)/shard_map/all_to_all | solution.py:20
  127.3 6.9 %copy-start.6 = (s32[1024]{0:T(1024)S(1)}, s32[1024]{0:T(1024)}, u32[]{:S(2)}) copy-start(s32[1024]{0:T(1024)} %param.5) | copy-start | bytes 12292
  130.8 10.1 %all-to-all-start.3 = ((f32[8,1,1024]{2,1,0:T(1,128)}), f32[8,1,1024]{2,1,0:T(1,128)S(1)}, u32[]{:S(2)}, u32[]{:S(2)}) async-start(f32[8,1,1024]{2,1,0:T(1,128)} %broadcast_in_dim.34), calls=%async_computation.3 | async-start | bytes 65536 | tf_op jit(solution)/shard_map/all_to_all | solution.py:20
  141.0 11.0 %copy-start.3 = (f32[1024,512]{1,0:T(8,128)S(1)}, f32[1024,512]{1,0:T(8,128)}, u32[]{:S(2)}) copy-start(f32[1024,512]{1,0:T(8,128)} %gather_fusion) | copy-start | bytes 6291460
  144.8 19.2 %all-to-all-start.4 = ((f32[64,1,1024]{2,1,0:T(1,128)}), f32[64,1,1024]{2,1,0:T(1,128)S(1)}, u32[]{:S(2)}, u32[]{:S(2)}) async-start(f32[64,1,1024]{2,1,0:T(1,128)} %broadcast_in_dim.35), calls=%async_computation.4 | async-start | bytes 524288 | tf_op jit(solution)/shard_map/all_to_all | solution.py:20
  152.0 84.4 %reduce-scatter.2.cloned.1.call-start = ((), (), s32[]{:S(2)}) async-start(), calls=%async_computation.11 | async-start | bytes 2359296 | tf_op jit(solution)/shard_map/reduce_scatter | solution.py:72
  164.2 14.7 %copy-start.2 = (f32[1024,512]{1,0:T(8,128)S(1)}, f32[1024,512]{1,0:T(8,128)}, u32[]{:S(2)}) copy-start(f32[1024,512]{1,0:T(8,128)} %all-gather.2.cloned.1.call-done) | copy-start | bytes 6291460
  167.9 10.9 %all-to-all-start.5 = ((f32[8,1,1024]{2,1,0:T(1,128)}), f32[8,1,1024]{2,1,0:T(1,128)S(1)}, u32[]{:S(2)}, u32[]{:S(2)}) async-start(f32[8,1,1024]{2,1,0:T(1,128)} %broadcast_in_dim.36), calls=%async_computation.5 | async-start | bytes 65536 | tf_op jit(solution)/shard_map/all_to_all | solution.py:20
  184.9 1.3 copy-start.4
  186.3 6.1 %collective-permute-start = (f32[32,8,1024]{2,1,0:T(8,128)S(1)}, f32[32,8,1024]{2,1,0:T(8,128)S(1)}, u32[]{:S(2)}, u32[]{:S(2)}) collective-permute-start(f32[32,8,1024]{2,1,0:T(8,128)S(1)} %dynamic-slice_bitcast_fusion), channel_id=1, source_target_pairs={{0,8},{8,0},{1,9},{9,1},{2,10},{10,2},{3,11},{11,3},{4,12},{12,4},... | collective-permute-start | bytes 3145736 | tf_op jit(solution)/shard_map/ppermute | solution.py:63
  194.8 18.4 %all-to-all-start.6 = ((f32[4,8,8,1024]{3,2,1,0:T(8,128)}), f32[4,8,8,1024]{3,2,1,0:T(8,128)S(1)}, u32[]{:S(2)}, u32[]{:S(2)}) async-start(f32[4,8,8,1024]{3,2,1,0:T(8,128)} %bitcast.3), calls=%async_computation.6 | async-start | bytes 2097152 | tf_op jit(solution)/shard_map/all_to_all | solution.py:24
  201.5 35.0 %copy-start.5 = (f32[128,512]{1,0:T(8,128)S(1)}, f32[128,512]{1,0:T(8,128)}, u32[]{:S(2)}) copy-start(f32[128,512]{1,0:T(8,128)} %param.3) | copy-start | bytes 786436
  214.1 18.5 %all-to-all-start.8 = ((f32[64,1,1024]{2,1,0:T(1,128)}), f32[64,1,1024]{2,1,0:T(1,128)S(1)}, u32[]{:S(2)}, u32[]{:S(2)}) async-start(f32[64,1,1024]{2,1,0:T(1,128)} %broadcast_in_dim.37), calls=%async_computation.8 | async-start | bytes 524288 | tf_op jit(solution)/shard_map/all_to_all | solution.py:20
  232.5 14.8 %all-to-all-start.7 = ((f32[8,8,1024]{2,1,0:T(8,128)}), f32[8,8,1024]{2,1,0:T(8,128)S(1)}, u32[]{:S(2)}, u32[]{:S(2)}) async-start(f32[8,8,1024]{2,1,0:T(8,128)} %reduce_sum.176), calls=%async_computation.7 | async-start | bytes 524288 | tf_op jit(solution)/shard_map/all_to_all | solution.py:24
Sparse Core Ops, SparseCore 0:
  10.1 46.0 all-gather.1
  155.7 39.9 reduce-scatter.1
where the time goes:
time: 256 us; the launch traced here: 255 us
  waiting for transfers between devices  112 us (44%)
  starting transfers between devices  39.9 us (16%)
  blocking collectives  36.8 us (14%)
  other arithmetic  29.7 us (12%)
  between operations  14.3 us (6%)
  matrix products  11.6 us (5%)
  local copies, waits for them, and re-layouts  10.5 us (4%)
    all_gather x1, waiting for transfers between devices, body(): gathered = lax.all_gather(items, 'code', axis=0, tiled=True)  46.3 us
    all_to_all x5, waiting for transfers between devices, exchange_sum(): return jnp.sum(lax.all_to_all(copies, axes, 0, 0), axis=0)  42.1 us
    all_to_all x2, blocking collectives, exchange_sum(): return jnp.sum(lax.all_to_all(copies, axes, 0, 0), axis=0)  36.8 us
    all_to_all x5, starting transfers between devices, exchange_sum(): return jnp.sum(lax.all_to_all(copies, axes, 0, 0), axis=0)  28.3 us
    all_to_all x2, waiting for transfers between devices, scatter_sum(): return jnp.sum(lax.all_to_all(blocks, axis, 0, 0), axis=0)  20.8 us
    reduce_sum x3, other arithmetic, body(): row_part = jnp.sum(kernel_vals * col_scale[None, :], axis=1)  8.8 us
    reduce_sum x3, other arithmetic, body(): col_part = jnp.sum(kernel_vals * row_scale[:, None], axis=0)  8.49 us
    all_to_all x2, starting transfers between devices, scatter_sum(): return jnp.sum(lax.all_to_all(blocks, axis, 0, 0), axis=0)  7.73 us
  transfers between devices with their start and end apart: 10, of which 9 were waited for; matrix products, arithmetic and copies ran while one was open for 11% of the time, Pallas kernels for 0%

commit v1 on v0

--- a/solution.py
+++ b/solution.py
@@ -31,7 +31,8 @@
     own_rows, width = items.shape
     total_items = own_rows * code_count * dp_count
     scaled = unit_rows(codewords) * (inverse_temp / width)
-    gathered = lax.all_gather(items, "code", axis=0, tiled=True)
+    stack = jnp.stack([items] * lax.axis_size("code"))
+    gathered = jnp.concatenate(lax.all_to_all(stack, "code", 0, 0), axis=0)
     logits = lax.dot_general(
         unit_rows(gathered),
         scaled,

time: 256 us -> 271 us (1.059)
  blocking collectives: 36.8 us -> 63.1 us
  waiting for transfers between devices: 112 us -> 94.2 us
  local copies, waits for them, and re-layouts: 10.5 us -> 16 us
    all_to_all x0 -> x1, waiting for transfers between devices: none -> 48.3 us  [body(): gathered = jnp.concatenate(lax.all_to_all(stack, 'code', 0, 0), axis=0)]
    all_gather x1 -> x0, waiting for transfers between devices: 46.3 us -> none  [body(): gathered = lax.all_gather(items, 'code', axis=0, tiled=True)]
    all_to_all x2 -> x4, blocking collectives: 36.8 us -> 63.1 us  [exchange_sum(): return jnp.sum(lax.all_to_all(copies, axes, 0, 0), axis=0)]
    all_to_all x5 -> x3, waiting for transfers between devices: 42.1 us -> 22.8 us  [exchange_sum(): return jnp.sum(lax.all_to_all(copies, axes, 0, 0), axis=0)]
    all_to_all x5 -> x3, starting transfers between devices: 28.3 us -> 17 us  [exchange_sum(): return jnp.sum(lax.all_to_all(copies, axes, 0, 0), axis=0)]
    all_to_all x0 -> x1, starting transfers between devices: none -> 11 us  [body(): gathered = jnp.concatenate(lax.all_to_all(stack, 'code', 0, 0), axis=0)]
    mul x0 -> x2, other arithmetic: none -> 3.34 us  [the longest x1 1.79 us: unit_rows(): values * lax.rsqrt(jnp.mean(values * values, axis=-1, keepdims=True) + ep...]
    dot_general x0 -> x1, local copies, waits for them, and re-layouts: none -> 2.95 us  [body(): lax.dot_general(row_scale[:, None] * gathered, kernel_vals, (((0,), (0,))...]
  transfers between devices with their start and end apart: 10 -> 8, of which waited for: 9 -> 7; matrix products, arithmetic and copies ran while one was open for 11% -> 10% of each run, Pallas kernels for 0% -> 0%
where the time goes in v1:
time: 271 us; the launch traced here: 270 us
  waiting for transfers between devices  94.2 us (35%)
  blocking collectives  63.1 us (23%)
  starting transfers between devices  39.4 us (15%)
  other arithmetic  30.9 us (11%)
  local copies, waits for them, and re-layouts  16 us (6%)
  between operations  14.3 us (5%)
  matrix products  11.9 us (4%)
    all_to_all x4, blocking collectives, exchange_sum(): return jnp.sum(lax.all_to_all(copies, axes, 0, 0), axis=0)  63.1 us
    all_to_all x1, waiting for transfers between devices, body(): gathered = jnp.concatenate(lax.all_to_all(stack, 'code', 0, 0), axis=0)  48.3 us
    all_to_all x3, waiting for transfers between devices, exchange_sum(): return jnp.sum(lax.all_to_all(copies, axes, 0, 0), axis=0)  22.8 us
    all_to_all x2, waiting for transfers between devices, scatter_sum(): return jnp.sum(lax.all_to_all(blocks, axis, 0, 0), axis=0)  20.7 us
    all_to_all x3, starting transfers between devices, exchange_sum(): return jnp.sum(lax.all_to_all(copies, axes, 0, 0), axis=0)  17 us
    all_to_all x1, starting transfers between devices, body(): gathered = jnp.concatenate(lax.all_to_all(stack, 'code', 0, 0), axis=0)  11 us
    reduce_sum x3, other arithmetic, body(): row_part = jnp.sum(kernel_vals * col_scale[None, :], axis=1)  8.79 us
    reduce_sum x3, other arithmetic, body(): col_part = jnp.sum(kernel_vals * row_scale[:, None], axis=0)  8.41 us
  transfers between devices with their start and end apart: 8, of which 7 were waited for; matrix products, arithmetic and copies ran while one was open for 10% of the time, Pallas kernels for 0%

profile of v1, /device:TPU:1, one launch (start us, length us, event | category | flops | bytes accessed | tf_op | source)
XLA Modules:
  0.0 269.8 jit_solution(4308165803321121156)
XLA Ops:
  9.7 11.0 %all-to-all-start = ((f32[8,128,512]{1,2,0:T(8,128)}), f32[8,128,512]{1,2,0:T(8,128)}, u32[]{:S(2)}, u32[]{:S(2)}) async-start(f32[8,128,512]{1,2,0:T(8,128)} %stack.2), calls=%async_computation | async-start | bytes 4194304 | tf_op jit(solution)/shard_map/all_to_all | solution.py:35
  20.9 48.3 %all-to-all-done = f32[8,128,512]{1,2,0:T(8,128)} async-done(((f32[8,128,512]{1,2,0:T(8,128)}), f32[8,128,512]{1,2,0:T(8,128)}, u32[]{:S(2)}, u32[]{:S(2)}) %all-to-all-start) | async-done | bytes 2097184 | tf_op jit(solution)/shard_map/all_to_all | solution.py:35
  70.9 2.9 %copy.17 = f32[8,128,512]{2,1,0:T(8,128)} copy(f32[8,128,512]{1,2,0:T(8,128)} %all-to-all-done) | data formatting | bytes 4194304 | tf_op jit(solution)/shard_map/all_to_all | solution.py:35
  75.7 5.6 %exponential_reduce_fusion = (f32[1024]{0:T(1024)S(1)}, f32[1024,1024]{1,0:T(8,128)}) fusion(f32[1024,512]{1,0:T(8,128)S(1)} %bitcast_multiply_fusion.1, f32[1024,512]{1,0:T(8,128)S(1)} %copy-done, f32[1024]{0:T(1024)S(1)} %add_rsqrt_fusion), kind=kOutput, calls=%fused_computation.10 | convolution fusion | flops 3223321600 | bytes 8396800 | tf_op jit(solution)/shard_map/dot_general | solution.py:36
  81.4 25.7 %all_to_all.57 = f32[64,1,1024]{2,1,0:T(1,128)S(1)} all-to-all(f32[64,1,1024]{2,1,0:T(1,128)S(1)} %broadcast_in_dim.31), channel_id=1, replica_groups=mesh['x'=4,'y'=8,'core'=2,'code'=8] {'x','y','core'}, dimensions={0} | all-to-all | bytes 524288 | tf_op jit(solution)/shard_map/all_to_all | solution.py:20
  110.2 9.2 %all_to_all.58 = f32[8,1,1024]{2,1,0:T(1,128)S(1)} all-to-all(f32[8,1,1024]{2,1,0:T(1,128)S(1)} %broadcast_in_dim.32), channel_id=1, replica_groups=mesh['x'=4,'y'=8,'core'=2,'code'=8] {'code'}, dimensions={0} | all-to-all | bytes 65536 | tf_op jit(solution)/shard_map/all_to_all | solution.py:20
  122.4 19.0 %all_to_all.59 = f32[64,1,1024]{2,1,0:T(1,128)S(1)} all-to-all(f32[64,1,1024]{2,1,0:T(1,128)S(1)} %broadcast_in_dim.33), channel_id=1, replica_groups=mesh['x'=4,'y'=8,'core'=2,'code'=8] {'x','y','core'}, dimensions={0} | all-to-all | bytes 524288 | tf_op jit(solution)/shard_map/all_to_all | solution.py:20
  141.5 2.9 %multiply_reduce_fusion.3 = f32[1024]{0:T(1024)S(1)} fusion(f32[1024,1024]{1,0:T(8,128)} %get-tuple-element.5, f32[1024]{0:T(1024)S(1)} %multiply_divide_fusion.3), kind=kLoop, calls=%fused_computation.6 | loop fusion | flops 2096128 | bytes 4202496 | tf_op jit(solution)/shard_map/reduce_sum | solution.py:47
  144.5 9.2 %all_to_all.60 = f32[8,1,1024]{2,1,0:T(1,128)S(1)} all-to-all(f32[8,1,1024]{2,1,0:T(1,128)S(1)} %broadcast_in_dim.34), channel_id=1, replica_groups=mesh['x'=4,'y'=8,'core'=2,'code'=8] {'code'}, dimensions={0} | all-to-all | bytes 65536 | tf_op jit(solution)/shard_map/all_to_all | solution.py:20
  157.4 7.2 %all-to-all-start.5 = ((f32[64,1,1024]{2,1,0:T(1,128)}), f32[64,1,1024]{2,1,0:T(1,128)S(1)}, u32[]{:S(2)}, u32[]{:S(2)}) async-start(f32[64,1,1024]{2,1,0:T(1,128)} %broadcast_in_dim.35), calls=%async_computation.5 | async-start | bytes 524288 | tf_op jit(solution)/shard_map/all_to_all | solution.py:20
  164.6 4.9 %gather_fusion = f32[1024,512]{1,0:T(8,128)} fusion(f32[1024,512]{1,0:T(8,128)S(1)} %copy-done, s32[1024]{0:T(1024)S(1)} %fusion.8), kind=kCustom, calls=%fused_computation | custom fusion | bytes 4198400 | tf_op jit(solution)/shard_map/jit(_take)/gather | solution.py:72
  169.5 7.1 %all-to-all-done.5 = f32[64,1,1024]{2,1,0:T(1,128)S(1)} async-done(((f32[64,1,1024]{2,1,0:T(1,128)}), f32[64,1,1024]{2,1,0:T(1,128)S(1)}, u32[]{:S(2)}, u32[]{:S(2)}) %all-to-all-start.5) | async-done | bytes 262176 | tf_op jit(solution)/shard_map/all_to_all | solution.py:20
  176.8 3.0 %multiply_reduce_fusion.1 = f32[1024]{0:T(1024)S(1)} fusion(f32[1024,1024]{1,0:T(8,128)} %get-tuple-element.5, f32[1024]{0:T(1024)S(1)} %multiply_divide_fusion.1), kind=kLoop, calls=%fused_computation.4 | loop fusion | flops 2096128 | bytes 4202496 | tf_op jit(solution)/shard_map/reduce_sum | solution.py:47
  180.4 3.3 %all-to-all-start.6 = ((f32[8,1,1024]{2,1,0:T(1,128)}), f32[8,1,1024]{2,1,0:T(1,128)S(1)}, u32[]{:S(2)}, u32[]{:S(2)}) async-start(f32[8,1,1024]{2,1,0:T(1,128)} %broadcast_in_dim.36), calls=%async_computation.6 | async-start | bytes 65536 | tf_op jit(solution)/shard_map/all_to_all | solution.py:20
  186.0 4.5 %all-to-all-done.6 = f32[8,1,1024]{2,1,0:T(1,128)S(1)} async-done(((f32[8,1,1024]{2,1,0:T(1,128)}), f32[8,1,1024]{2,1,0:T(1,128)S(1)}, u32[]{:S(2)}, u32[]{:S(2)}) %all-to-all-start.6) | async-done | bytes 32800 | tf_op jit(solution)/shard_map/all_to_all | solution.py:20
  192.2 3.0 %copy.24 = f32[512,1024]{1,0:T(8,128)} copy(f32[512,1024]{0,1:T(8,128)} %bitcast.22) | data formatting | bytes 4194304 | tf_op jit(solution)/shard_map/dot_general | solution.py:53
  195.1 6.3 %fusion = f32[32,2,8,1024]{3,2,1,0:T(8,128)S(1)} fusion(f32[32,2,8,1024]{3,2,1,0:T(8,128)} %bitcast.21, f32[1024,1024]{1,0:T(8,128)} %get-tuple-element.5), kind=kOutput, calls=%fused_computation.1 | convolution fusion | flops 3221225472 | bytes 8388608 | tf_op jit(solution)/shard_map/dot_general | solution.py:53
  201.6 3.5 %collective-permute-start = (f32[32,8,1024]{2,1,0:T(8,128)S(1)}, f32[32,8,1024]{2,1,0:T(8,128)}, u32[]{:S(2)}, u32[]{:S(2)}) collective-permute-start(f32[32,8,1024]{2,1,0:T(8,128)S(1)} %dynamic-slice_bitcast_fusion), channel_id=1, source_target_pairs={{0,8},{8,0},{1,9},{9,1},{2,10},{10,2},{3,11},{11,3},{4,12},{12,4},... | collective-permute-start | bytes 3145736 | tf_op jit(solution)/shard_map/ppermute | solution.py:64
  209.9 3.7 %all-to-all-start.7 = ((f32[4,8,8,1024]{3,2,1,0:T(8,128)}), f32[4,8,8,1024]{3,2,1,0:T(8,128)S(1)}, u32[]{:S(2)}, u32[]{:S(2)}) async-start(f32[4,8,8,1024]{3,2,1,0:T(8,128)} %bitcast.8), calls=%async_computation.7 | async-start | bytes 2097152 | tf_op jit(solution)/shard_map/all_to_all | solution.py:24
  216.5 11.7 %all-to-all-done.7 = f32[4,8,8,1024]{3,2,1,0:T(8,128)S(1)} async-done(((f32[4,8,8,1024]{3,2,1,0:T(8,128)}), f32[4,8,8,1024]{3,2,1,0:T(8,128)S(1)}, u32[]{:S(2)}, u32[]{:S(2)}) %all-to-all-start.7) | async-done | bytes 1048608 | tf_op jit(solution)/shard_map/all_to_all | solution.py:24
  229.0 6.5 %all-to-all-start.9 = ((f32[64,1,1024]{2,1,0:T(1,128)}), f32[64,1,1024]{2,1,0:T(1,128)S(1)}, u32[]{:S(2)}, u32[]{:S(2)}) async-start(f32[64,1,1024]{2,1,0:T(1,128)} %broadcast_in_dim.37), calls=%async_computation.9 | async-start | bytes 524288 | tf_op jit(solution)/shard_map/all_to_all | solution.py:20
  236.3 11.2 %all-to-all-done.9 = f32[64,1,1024]{2,1,0:T(1,128)S(1)} async-done(((f32[64,1,1024]{2,1,0:T(1,128)}), f32[64,1,1024]{2,1,0:T(1,128)S(1)}, u32[]{:S(2)}, u32[]{:S(2)}) %all-to-all-start.9) | async-done | bytes 262176 | tf_op jit(solution)/shard_map/all_to_all | solution.py:20
  247.5 3.9 %all-to-all-start.8 = ((f32[8,8,1024]{2,1,0:T(8,128)}), f32[8,8,1024]{2,1,0:T(8,128)S(1)}, u32[]{:S(2)}, u32[]{:S(2)}) async-start(f32[8,8,1024]{2,1,0:T(8,128)} %reduce_sum.176), calls=%async_computation.8 | async-start | bytes 524288 | tf_op jit(solution)/shard_map/all_to_all | solution.py:24
  253.3 9.0 %all-to-all-done.8 = f32[8,8,1024]{2,1,0:T(8,128)S(1)} async-done(((f32[8,8,1024]{2,1,0:T(8,128)}), f32[8,8,1024]{2,1,0:T(8,128)S(1)}, u32[]{:S(2)}, u32[]{:S(2)}) %all-to-all-start.8) | async-done | bytes 262176 | tf_op jit(solution)/shard_map/all_to_all | solution.py:24
  (55 shorter events, 32.9 us)
Async XLA Ops:
  9.7 11.0 %copy-start = (f32[1024,512]{1,0:T(8,128)S(1)}, f32[1024,512]{1,0:T(8,128)}, u32[]{:S(2)}) copy-start(f32[1024,512]{1,0:T(8,128)} %param.4) | copy-start | bytes 6291460
  9.7 59.5 %all-to-all-start = ((f32[8,128,512]{1,2,0:T(8,128)}), f32[8,128,512]{1,2,0:T(8,128)}, u32[]{:S(2)}, u32[]{:S(2)}) async-start(f32[8,128,512]{1,2,0:T(8,128)} %stack.2), calls=%async_computation | async-start | bytes 4194304 | tf_op jit(solution)/shard_map/all_to_all | solution.py:35
  153.7 10.8 %copy-start.4 = (s32[1024]{0:T(1024)S(1)}, s32[1024]{0:T(1024)}, u32[]{:S(2)}) copy-start(s32[1024]{0:T(1024)} %param.5) | copy-start | bytes 12292
  157.4 19.2 %all-to-all-start.5 = ((f32[64,1,1024]{2,1,0:T(1,128)}), f32[64,1,1024]{2,1,0:T(1,128)S(1)}, u32[]{:S(2)}, u32[]{:S(2)}) async-start(f32[64,1,1024]{2,1,0:T(1,128)} %broadcast_in_dim.35), calls=%async_computation.5 | async-start | bytes 524288 | tf_op jit(solution)/shard_map/all_to_all | solution.py:20
  176.8 7.3 %copy-start.2 = (f32[1024,512]{1,0:T(8,128)S(1)}, f32[1024,512]{1,0:T(8,128)}, u32[]{:S(2)}) copy-start(f32[1024,512]{1,0:T(8,128)} %gather_fusion) | copy-start | bytes 6291460
  180.4 10.1 %all-to-all-start.6 = ((f32[8,1,1024]{2,1,0:T(1,128)}), f32[8,1,1024]{2,1,0:T(1,128)S(1)}, u32[]{:S(2)}, u32[]{:S(2)}) async-start(f32[8,1,1024]{2,1,0:T(1,128)} %broadcast_in_dim.36), calls=%async_computation.6 | async-start | bytes 65536 | tf_op jit(solution)/shard_map/all_to_all | solution.py:20
  183.8 67.6 %reduce-scatter.2.cloned.1.call-start = ((), (), s32[]{:S(2)}) async-start(), calls=%async_computation.11 | async-start | bytes 2359296 | tf_op jit(solution)/shard_map/reduce_scatter | solution.py:73
  186.0 4.6 %copy-start.1 = (f32[8,128,512]{2,1,0:T(8,128)S(1)}, f32[8,128,512]{2,1,0:T(8,128)}, u32[]{:S(2)}) copy-start(f32[8,128,512]{2,1,0:T(8,128)} %copy.17) | copy-start | bytes 6291460
  201.6 5.9 %collective-permute-start = (f32[32,8,1024]{2,1,0:T(8,128)S(1)}, f32[32,8,1024]{2,1,0:T(8,128)}, u32[]{:S(2)}, u32[]{:S(2)}) collective-permute-start(f32[32,8,1024]{2,1,0:T(8,128)S(1)} %dynamic-slice_bitcast_fusion), channel_id=1, source_target_pairs={{0,8},{8,0},{1,9},{9,1},{2,10},{10,2},{3,11},{11,3},{4,12},{12,4},... | collective-permute-start | bytes 3145736 | tf_op jit(solution)/shard_map/ppermute | solution.py:64
  209.9 18.3 %all-to-all-start.7 = ((f32[4,8,8,1024]{3,2,1,0:T(8,128)}), f32[4,8,8,1024]{3,2,1,0:T(8,128)S(1)}, u32[]{:S(2)}, u32[]{:S(2)}) async-start(f32[4,8,8,1024]{3,2,1,0:T(8,128)} %bitcast.8), calls=%async_computation.7 | async-start | bytes 2097152 | tf_op jit(solution)/shard_map/all_to_all | solution.py:24
  216.5 34.9 %copy-start.3 = (f32[128,512]{1,0:T(8,128)S(1)}, f32[128,512]{1,0:T(8,128)}, u32[]{:S(2)}) copy-start(f32[128,512]{1,0:T(8,128)} %param.3) | copy-start | bytes 786436
  229.0 18.5 %all-to-all-start.9 = ((f32[64,1,1024]{2,1,0:T(1,128)}), f32[64,1,1024]{2,1,0:T(1,128)S(1)}, u32[]{:S(2)}, u32[]{:S(2)}) async-start(f32[64,1,1024]{2,1,0:T(1,128)} %broadcast_in_dim.37), calls=%async_computation.9 | async-start | bytes 524288 | tf_op jit(solution)/shard_map/all_to_all | solution.py:20
  247.5 14.8 %all-to-all-start.8 = ((f32[8,8,1024]{2,1,0:T(8,128)}), f32[8,8,1024]{2,1,0:T(8,128)S(1)}, u32[]{:S(2)}, u32[]{:S(2)}) async-start(f32[8,8,1024]{2,1,0:T(8,128)} %reduce_sum.176), calls=%async_computation.8 | async-start | bytes 524288 | tf_op jit(solution)/shard_map/all_to_all | solution.py:24
Sparse Core Ops, SparseCore 0:
  187.5 37.9 reduce-scatter.1
